TPU v7x, 128 devices: a whole 4x4x4 slice. The times are simulated.
128 devices in a mesh: rep: 8 (over x_hi, y), gx: 4 (over x_lo, core), gy: 4 (over z).
Axes of the slice: x: 4 (x_hi: 2, x_lo: 2; x = x_hi * 2 + x_lo), y: 4, z: 4, core: 2. Of those that a mesh axis runs over, the one named last changes fastest.
Arguments:
- deltas: bfloat16 [8, 2, 3584, 14336], P('rep', None, 'gx', 'gy'), may hold values from -32 to 32
- params: float32 [2, 4, 4, 8, 4, 4, 28, 896], P(None, None, 'gx', 'rep', None, 'gy'), may hold values from -0.75 to 0.75
- momentum: float32 [2, 4, 4, 8, 4, 4, 28, 896], P(None, None, 'gx', 'rep', None, 'gy'), may hold values from -1.5 to 1.5
Outputs:
- new_params: float32 [2, 4, 4, 8, 4, 4, 28, 896], P(None, None, 'gx', 'rep', None, 'gy')
- new_momentum: float32 [2, 4, 4, 8, 4, 4, 28, 896], P(None, None, 'gx', 'rep', None, 'gy')
All inputs are finite; a program needn't handle non-finite values.
Results may differ from a plain program's by a relative error of at most 0.0003.
Values may be sent and summed in bfloat16 or wider, within the bound.
No kernel may reach another device: no remote copies, remote signals or barrier semaphores. Data moves between devices by JAX's collectives and lax.ppermute only.
A program may use at most 128 MiB of HBM per device.

v0:
```python
import jax
import jax.numpy as jnp
from jax import lax
from jax.sharding import Mesh
from jax.sharding import PartitionSpec as P

GX = ("gx_0", "gx_1")
REP = ("rep_0", "rep_1")
REP_GX_GY = ("rep_0", "rep_1", "gx_0", "gx_1", "gy")
GX_GY = ("gx_0", "gx_1", "gy")


clip_level = 0.25
moment_decay = 0.9
outer_rate = 0.7
epsilon = 1e-06


def over_axes(x, axes):
    for axis in axes:
        x = lax.psum(x, axis)
    return x


def split_up(x, dim, devices):
    lengths = x.shape
    pieces = x.reshape(*lengths[:dim], devices, lengths[dim] // devices, *lengths[dim + 1 :])
    return jnp.moveaxis(pieces, dim, 0)


def laid_out(pieces, dim):
    pieces = jnp.moveaxis(pieces, 0, dim)
    lengths = pieces.shape
    return pieces.reshape(*lengths[:dim], lengths[dim] * lengths[dim + 1], *lengths[dim + 2 :])


def joined_exchange(x, axis, axes, splits, concats):
    sizes = [lax.axis_size(a) for a in axes]
    pieces = split_up(x, splits[0], sizes[0])
    pieces = jnp.moveaxis(split_up(pieces, splits[1] + 1, sizes[1]), 0, 1)
    inside = pieces.shape[2:]
    pieces = pieces.reshape(-1, *inside)
    pieces = lax.all_to_all(pieces, axis, split_axis=0, concat_axis=0, tiled=True)
    pieces = laid_out(pieces.reshape(*sizes, *inside), concats[0] + 1)
    return laid_out(pieces, concats[1])


def per_device(deltas, params, momentum):
    rows_split = lax.axis_size(GX)
    cols_split = lax.axis_size("gy")
    replicas = lax.axis_size(REP)
    matrices = deltas.shape[1]
    local_rows = deltas.shape[2]
    local_cols = deltas.shape[3]
    row_tile = local_rows // (rows_split * replicas)
    col_tile = local_cols // cols_split
    entries = matrices * local_rows * local_cols * rows_split * cols_split
    blocks = deltas.reshape(matrices, rows_split, replicas, row_tile, cols_split, col_tile)
    received = lax.all_to_all(blocks[None], REP, split_axis=3, concat_axis=0, tiled=True)
    summed = jnp.sum(received, axis=0, dtype=jnp.float32)
    partial_value = summed / replicas
    squares = over_axes(jnp.sum(partial_value * partial_value), REP_GX_GY)
    mean_delta = joined_exchange(partial_value, GX_GY, (GX, "gy"), (1, 4), (1, 4))
    root_mean = jnp.sqrt(squares / entries + epsilon)
    clip_scale = jnp.minimum(1.0, clip_level / root_mean)
    arranged = jnp.transpose(mean_delta, (0, 1, 2, 4, 3, 5)).reshape(params.shape)
    gradient = clip_scale * arranged
    new_momentum = moment_decay * momentum + gradient
    new_params = params - outer_rate * (gradient + moment_decay * new_momentum)
    return (new_params, new_momentum)


def solution(mesh):
    finer = Mesh(
        mesh.devices.reshape(2, 4, 2, 2, mesh.shape["gy"]), ("rep_0", "rep_1", "gx_0", "gx_1", "gy")
    )
    return jax.shard_map(
        per_device,
        mesh=finer,
        in_specs=(
            P(REP, None, GX, "gy"),
            P(None, None, GX, REP, None, "gy", None, None),
            P(None, None, GX, REP, None, "gy", None, None),
        ),
        out_specs=(
            P(None, None, GX, REP, None, "gy", None, None),
            P(None, None, GX, REP, None, "gy", None, None),
        ),
        check_vma=False,
    )
```

profile of v0, /device:TPU:1, one launch (start us, length us, event | category | flops | bytes accessed | tf_op | source)
XLA Modules:
  0.0 291.2 jit_solution(4495776960698477434)
XLA Ops:
  0.6 21.9 %broadcast_in_dim_reshape.3 = bf16[1,2,4,8,28,4,896]{6,5,4,3,2,1,0:T(4,128)(2,1)} reshape(bf16[1,2,896,3584]{3,2,1,0:T(8,128)(2,1)} %param.3) | data formatting | bytes 25690112 | tf_op jit(solution)/shard_map/broadcast_in_dim;reshape | solution.py:59
  22.5 6.3 %copy.31 = bf16[1,2,4,8,28,4,896]{6,5,4,2,1,0,3:T(4,128)(2,1)S(1)} copy(bf16[1,2,4,8,28,4,896]{6,5,4,3,2,1,0:T(4,128)(2,1)} %broadcast_in_dim_reshape.3) | data formatting | bytes 25690112 | tf_op jit(solution)/shard_map/broadcast_in_dim;reshape | solution.py:59
  28.8 149.3 %all_to_all.14 = bf16[1,2,4,8,28,4,896]{6,5,4,2,1,0,3:T(4,128)(2,1)S(1)} all-to-all(bf16[1,2,4,8,28,4,896]{6,5,4,2,1,0,3:T(4,128)(2,1)S(1)} %copy.31), channel_id=1, replica_groups=mesh['rep_0'=2,'rep_1'=4,'gx_0'=2,'gx_1'=2,'gy'=4] {'rep_0','rep_1'}, dimensions={3} | all-to-all | bytes 25690112 | tf_op jit(solution)/shard_map/all_to_all | solution.py:59
  178.1 15.3 %convert_reduce_fusion = f32[2,4,28,4,896]{4,3,2,1,0:T(4,128)S(1)} fusion(bf16[1,2,4,8,28,4,896]{6,5,4,2,1,0,3:T(4,128)(2,1)S(1)} %all_to_all.14), kind=kLoop, calls=%fused_computation | loop fusion | flops 12042240 | bytes 16056320 | tf_op jit(solution)/shard_map/reduce_sum | solution.py:60
  193.3 2.3 multiply_reduce_fusion
  195.6 4.2 %copy.34 = f32[4,4,2,1,1,28,1,896]{7,2,5,1,0,6,4,3:T(2,128)} copy(f32[4,4,2,1,1,28,1,896]{7,1,5,0,2,6,4,3:T(4,128)S(1)} %get-tuple-element.15) | data formatting | bytes 6422528 | tf_op jit(solution)/shard_map/transpose;transpose | solution.py:40
  199.8 9.8 %all-to-all-start.1 = ((f32[16,2,1,1,28,1,896]{6,1,4,5,3,2,0:T(2,128)}), f32[16,2,1,1,28,1,896]{6,1,4,5,3,2,0:T(2,128)S(1)}, u32[]{:S(2)}, u32[]{:S(2)}) async-start(f32[16,2,1,1,28,1,896]{6,1,4,5,3,2,0:T(2,128)} %bitcast.36), calls=%async_computation.1 | async-start | bytes 6422528 | tf_op jit(solution)/shard_map/all_to_all | solution.py:43
  209.6 38.7 %psum.35 = f32[]{:T(128)} all-reduce(f32[]{:T(128)} %get-tuple-element.14), channel_id=1, replica_groups=mesh['rep_0'=2,'rep_1'=4,'gx_0'=2,'gx_1'=2,'gy'=4] {'rep_0'}, use_global_device_ids=true, to_apply=%region_2.0 | all-reduce | flops 1 | bytes 8 | tf_op jit(solution)/shard_map/psum | solution.py:21
  248.3 7.2 %psum.36 = f32[]{:T(128)} all-reduce(f32[]{:T(128)} %psum.35), channel_id=1, replica_groups=mesh['rep_0'=2,'rep_1'=4,'gx_0'=2,'gx_1'=2,'gy'=4] {'rep_1'}, use_global_device_ids=true, to_apply=%region_3.0 | all-reduce | flops 1 | bytes 8 | tf_op jit(solution)/shard_map/psum | solution.py:21
  255.5 4.4 %psum.37 = f32[]{:T(128)} all-reduce(f32[]{:T(128)} %psum.36), channel_id=1, replica_groups=mesh['rep_0'=2,'rep_1'=4,'gx_0'=2,'gx_1'=2,'gy'=4] {'gx_0'}, use_global_device_ids=true, to_apply=%region_4.0 | all-reduce | flops 1 | bytes 8 | tf_op jit(solution)/shard_map/psum | solution.py:21
  259.9 6.6 %psum.38 = f32[]{:T(128)} all-reduce(f32[]{:T(128)} %psum.37), channel_id=1, replica_groups=mesh['rep_0'=2,'rep_1'=4,'gx_0'=2,'gx_1'=2,'gy'=4] {'gx_1'}, use_global_device_ids=true, to_apply=%region_5.0 | all-reduce | flops 1 | bytes 8 | tf_op jit(solution)/shard_map/psum | solution.py:21
  266.5 8.9 %psum.39 = f32[]{:T(128)} all-reduce(f32[]{:T(128)} %psum.38), channel_id=1, replica_groups=mesh['rep_0'=2,'rep_1'=4,'gx_0'=2,'gx_1'=2,'gy'=4] {'gy'}, use_global_device_ids=true, to_apply=%region_6.0 | all-reduce | flops 1 | bytes 8 | tf_op jit(solution)/shard_map/psum | solution.py:21
  276.1 0.0 all-to-all-done.1
  276.1 0.0 copy-start
  276.1 0.0 copy-start.1
  276.1 0.2 broadcast_multiply_fusion
  276.3 1.7 copy-done
  278.0 1.0 copy-done.1
  279.0 2.3 bitcast_add_fusion.1
  281.3 5.0 %copy.40 = f32[2,4,1,1,4,1,28,896]{7,5,6,4,3,2,1,0:T(1,128)} copy(f32[2,4,1,1,4,1,28,896]{7,4,6,1,0,5,3,2:T(4,128)S(1)} %get-tuple-element.12) | data formatting | bytes 6422528
  286.2 5.0 %copy.39 = f32[2,4,1,1,4,1,28,896]{7,5,6,4,3,2,1,0:T(1,128)} copy(f32[2,4,1,1,4,1,28,896]{7,4,6,1,0,5,3,2:T(4,128)S(1)} %get-tuple-element.13) | data formatting | bytes 6422528
Async XLA Ops:
  199.8 76.3 %all-to-all-start.1 = ((f32[16,2,1,1,28,1,896]{6,1,4,5,3,2,0:T(2,128)}), f32[16,2,1,1,28,1,896]{6,1,4,5,3,2,0:T(2,128)S(1)}, u32[]{:S(2)}, u32[]{:S(2)}) async-start(f32[16,2,1,1,28,1,896]{6,1,4,5,3,2,0:T(2,128)} %bitcast.36), calls=%async_computation.1 | async-start | bytes 6422528 | tf_op jit(solution)/shard_map/all_to_all | solution.py:43
  276.1 1.9 copy-start
  276.1 2.9 copy-start.1
where the time goes:
time: 293 us; the launch traced here: 291 us
  blocking collectives  215 us (73%)
  local copies, waits for them, and re-layouts  45 us (15%)
  other arithmetic  20 us (7%)
  starting transfers between devices  9.84 us (3%)
    all_to_all x1, blocking collectives, per_device(): lax.all_to_all(blocks[None], REP, split_axis=3, concat_axis=0, tiled=True)  149 us
    psum x5, blocking collectives, over_axes(): x = lax.psum(x, axis)  65.8 us
    another operation x2, local copies, waits for them, and re-layouts, per_device(): blocks[None]  28.2 us
    reduce_sum x1, other arithmetic, per_device(): summed = jnp.sum(received, axis=0, dtype=jnp.float32)  15.3 us
    unnamed x6, local copies, waits for them, and re-layouts  12.6 us
    all_to_all x1, starting transfers between devices, joined_exchange(): lax.all_to_all(pieces, axis, split_axis=0, concat_axis=0, tiled=True)  9.84 us
  transfers between devices with their start and end apart: 1, of which 0 were waited for; matrix products, arithmetic and copies ran while one was open for 0% of the time, Pallas kernels for 0%

commit v1 on v0

v1 whole, which is shorter than its diff:
```python
import jax
import jax.numpy as jnp
from jax import lax
from jax.experimental import pallas as pl
from jax.experimental.pallas import tpu as pltpu
from jax.sharding import Mesh
from jax.sharding import PartitionSpec as P

GX = ("gx_0", "gx_1")
REP = ("rep_0", "rep_1")
EVERY = ("rep_0", "rep_1", "gx_0", "gx_1", "gy")
LANES = 128

clip_level = 0.25
moment_decay = 0.9
outer_rate = 0.7
epsilon = 1e-06


def pack_kernel(replicas, row_tile, x_ref, out_ref):
    for r in range(replicas):
        for m in range(2):
            out_ref[r, 0, 0, m * row_tile : (m + 1) * row_tile, :] = x_ref[
                m, r * row_tile : (r + 1) * row_tile, :
            ]


def pack(deltas, replicas, rows_split, cols_split, row_tile, col_tile):
    block_rows = replicas * row_tile
    return pl.pallas_call(
        lambda x_ref, out_ref: pack_kernel(replicas, row_tile, x_ref, out_ref),
        name="pack",
        grid=(rows_split, cols_split),
        in_specs=[pl.BlockSpec((2, block_rows, col_tile), lambda c, d: (0, c, d))],
        out_specs=pl.BlockSpec(
            (replicas, 1, 1, 2 * row_tile, col_tile), lambda c, d: (0, c, d, 0, 0)
        ),
        out_shape=jax.ShapeDtypeStruct(
            (replicas, rows_split, cols_split, 2 * row_tile, col_tile), deltas.dtype
        ),
        compiler_params=pltpu.CompilerParams(vmem_limit_bytes=24 << 20),
    )(deltas)


def mean_kernel(replicas, blocks, row_tile, col_tile, x_ref, mean_ref, squares_ref):
    lane_tiles = col_tile // LANES
    squares_ref[...] = jnp.zeros_like(squares_ref)

    def block(ab, carry):
        for group in range(2 * row_tile // 8):
            total = x_ref[0, ab, group * 8 : group * 8 + 8, :].astype(jnp.float32)
            for replica in range(1, replicas):
                total = total + x_ref[
                    replica, ab, group * 8 : group * 8 + 8, :
                ].astype(jnp.float32)
            mean = total * (1.0 / replicas)
            square = mean * mean
            partial = square[:, :LANES]
            for j in range(1, lane_tiles):
                partial = partial + square[:, j * LANES : (j + 1) * LANES]
            squares_ref[...] += partial
            row = 0
            while row < 8:
                at = group * 8 + row
                m, i = at // row_tile, at % row_tile
                count = min(8 - row, row_tile - i)
                start = ((m * blocks + ab) * row_tile + i) * lane_tiles
                for j in range(lane_tiles):
                    mean_ref[pl.ds(start + j, count, stride=lane_tiles), :] = mean[
                        row : row + count, j * LANES : (j + 1) * LANES
                    ]
                row += count
        return carry

    lax.fori_loop(0, blocks, block, 0)


def average(received, row_tile, col_tile):
    replicas, blocks = received.shape[:2]
    size = blocks * 2 * row_tile * col_tile
    return pl.pallas_call(
        lambda *refs: mean_kernel(replicas, blocks, row_tile, col_tile, *refs),
        name="average",
        in_specs=[pl.BlockSpec(memory_space=pltpu.VMEM)],
        out_specs=[pl.BlockSpec(memory_space=pltpu.VMEM)] * 2,
        out_shape=[
            jax.ShapeDtypeStruct((size // LANES, LANES), jnp.float32),
            jax.ShapeDtypeStruct((8, LANES), jnp.float32),
        ],
        compiler_params=pltpu.CompilerParams(vmem_limit_bytes=24 << 20),
    )(received)


def step_kernel(entries, squares_ref, mean_ref, params_ref, momentum_ref, params_out, momentum_out):
    squares = jnp.sum(squares_ref[...], keepdims=True)
    root_mean = jnp.sqrt(squares * (1.0 / entries) + epsilon)
    clip_scale = jnp.minimum(1.0, clip_level / root_mean)
    gradient = clip_scale * mean_ref[...]
    momentum = moment_decay * momentum_ref[...] + gradient
    momentum_out[...] = momentum
    params_out[...] = params_ref[...] - outer_rate * (gradient + moment_decay * momentum)


def step(squares, mean, params, momentum, entries):
    rows = mean.shape[0]
    pieces = 8
    whole = pl.BlockSpec(squares.shape, lambda i: (0, 0))
    tile = pl.BlockSpec((rows // pieces, LANES), lambda i: (i, 0))
    return pl.pallas_call(
        lambda *refs: step_kernel(entries, *refs),
        name="outer_step",
        grid=(pieces,),
        in_specs=[whole, tile, tile, tile],
        out_specs=[tile, tile],
        out_shape=[jax.ShapeDtypeStruct(mean.shape, jnp.float32)] * 2,
        compiler_params=pltpu.CompilerParams(vmem_limit_bytes=16 << 20),
    )(squares, mean, params, momentum)


def per_device(deltas, params, momentum):
    rows_split = lax.axis_size(GX)
    cols_split = lax.axis_size("gy")
    replicas = lax.axis_size(REP)
    devices = rows_split * cols_split * replicas
    matrices, local_rows, local_cols = deltas.shape[1:]
    row_tile = local_rows // (rows_split * replicas)
    col_tile = local_cols // cols_split
    entries = matrices * local_rows * local_cols * rows_split * cols_split
    packed = pack(deltas[0], replicas, rows_split, cols_split, row_tile, col_tile)
    packed = packed.reshape(devices, 2 * row_tile, col_tile)
    received = lax.all_to_all(packed, EVERY, split_axis=0, concat_axis=0, tiled=True)
    received = received.reshape(replicas, rows_split * cols_split, 2 * row_tile, col_tile)
    mean, squares = average(received, row_tile, col_tile)
    squares = jnp.sum(squares, axis=0, keepdims=True)
    squares = jnp.broadcast_to(squares[None], (devices, 1, LANES))
    squares = lax.all_to_all(squares, EVERY, split_axis=0, concat_axis=0, tiled=True)
    flat = mean.shape
    new_params, new_momentum = step(
        squares.reshape(devices, LANES), mean, params.reshape(flat), momentum.reshape(flat), entries
    )
    return new_params.reshape(params.shape), new_momentum.reshape(params.shape)


def solution(mesh):
    finer = Mesh(
        mesh.devices.reshape(2, 4, 2, 2, mesh.shape["gy"]), ("rep_0", "rep_1", "gx_0", "gx_1", "gy")
    )
    return jax.shard_map(
        per_device,
        mesh=finer,
        in_specs=(
            P(REP, None, GX, "gy"),
            P(None, None, GX, REP, None, "gy", None, None),
            P(None, None, GX, REP, None, "gy", None, None),
        ),
        out_specs=(
            P(None, None, GX, REP, None, "gy", None, None),
            P(None, None, GX, REP, None, "gy", None, None),
        ),
        check_vma=False,
    )
```

time: 293 us -> 195 us (0.67)
  blocking collectives: 215 us -> 173 us
  local copies, waits for them, and re-layouts: 45 us -> 10.2 us
  other arithmetic: 20 us -> 0.02 us
  Pallas kernels: 0 us -> 10.5 us
  starting transfers between devices: 9.84 us -> 0 us
    psum x5 -> x0, blocking collectives: 65.8 us -> none  [over_axes(): x = lax.psum(x, axis)]
    another operation x3 -> x0, local copies, waits for them, and re-layouts: 32.3 us -> none  [the longest x2 28.2 us: per_device(): blocks[None]]
    all_to_all x1 -> x2, blocking collectives: 149 us -> 173 us  [the longest x1 157 us: per_device(): lax.all_to_all(packed, EVERY, split_axis=0, concat_axis=0, tiled=True)]
    reduce_sum x2 -> x1, other arithmetic: 17.5 us -> 0.02 us  [per_device(): squares = jnp.sum(squares, axis=0, keepdims=True)]
    pallas_call x0 -> x3, Pallas kernels: none -> 10.5 us  [the longest x1 4.71 us: step(): pl.pallas_call(lambda *refs: step_kernel(entries, *refs), name='outer_ste...]
    all_to_all x1 -> x0, starting transfers between devices: 9.84 us -> none  [joined_exchange(): lax.all_to_all(pieces, axis, split_axis=0, concat_axis=0, tiled=True)]
    unnamed x6 -> x10, local copies, waits for them, and re-layouts: 12.6 us -> 10.1 us
  transfers between devices with their start and end apart: 1 -> 0, of which waited for: 0 -> 0; matrix products, arithmetic and copies ran while one was open for 0% -> 0% of each run, Pallas kernels for 0% -> 0%
where the time goes in v1:
time: 195 us
  blocking collectives  173 us (89%)
  Pallas kernels  10.5 us (5%)
  local copies, waits for them, and re-layouts  10.2 us (5%)
    all_to_all x1, blocking collectives, per_device(): lax.all_to_all(packed, EVERY, split_axis=0, concat_axis=0, tiled=True)  157 us
    all_to_all x1, blocking collectives, per_device(): lax.all_to_all(squares, EVERY, split_axis=0, concat_axis=0, tiled=True)  16.5 us
    unnamed x10, local copies, waits for them, and re-layouts  10.1 us
    pallas_call x1, Pallas kernels, step(): pl.pallas_call(lambda *refs: step_kernel(entries, *refs), name='outer_ste...  4.71 us

profile of v1, /device:TPU:1, one launch (start us, length us, event | category | flops | bytes accessed | tf_op | source)
XLA Modules:
  0.0 194.6 jit_solution(11981972336087160705)
XLA Ops:
  0.6 0.0 copy-start
  0.6 4.6 %copy-done = bf16[1,2,896,3584]{3,2,1,0:T(8,128)(2,1)S(1)} copy-done((bf16[1,2,896,3584]{3,2,1,0:T(8,128)(2,1)S(1)}, bf16[1,2,896,3584]{3,2,1,0:T(8,128)(2,1)}, u32[]{:S(2)}) %copy-start) | copy-done | bytes 12845080
  5.3 3.8 %pack.1 = bf16[8,4,4,56,896]{4,3,2,1,0:T(8,128)(2,1)S(1)} custom-call(bf16[2,896,3584]{2,1,0:T(8,128)(2,1)S(1)} %bitcast.10), custom_call_target="tpu_custom_call" | custom-call | tf_op jit(solution)/shard_map/pack/pallas_call | solution.py:30
  9.1 156.8 %all_to_all.10 = bf16[128,56,896]{2,1,0:T(8,128)(2,1)S(1)} all-to-all(bf16[128,56,896]{2,1,0:T(8,128)(2,1)S(1)} %bitcast.9), channel_id=1, replica_groups=mesh['rep_0'=2,'rep_1'=4,'gx_0'=2,'gx_1'=2,'gy'=4] {'rep_0','rep_1','gx_..., dimensions={0} | all-to-all | bytes 25690112 | tf_op jit(solution)/shard_map/all_to_all | solution.py:131
  165.9 0.0 copy-start.1
  165.9 2.0 %average.1 = (f32[6272,128]{1,0:T(8,128)S(1)}, f32[8,128]{1,0:T(8,128)S(1)}) custom-call(bf16[8,16,56,896]{3,2,1,0:T(8,128)(2,1)S(1)} %bitcast.8), custom_call_target="tpu_custom_call" | custom-call | tf_op jit(solution)/shard_map/average/pallas_call | solution.py:81
  167.9 0.0 copy-start.3
  167.9 1.7 copy-done.3
  169.6 16.5 %all_to_all.11 = f32[128,1,128]{2,1,0:T(1,128)S(1)} all-to-all(f32[128,1,128]{2,1,0:T(1,128)S(1)} %broadcast_in_dim.2), channel_id=1, replica_groups=mesh['rep_0'=2,'rep_1'=4,'gx_0'=2,'gx_1'=2,'gy'=4] {'rep_0','rep_1','gx_..., dimensions={0} | all-to-all | bytes 131072 | tf_op jit(solution)/shard_map/all_to_all | solution.py:136
  186.1 0.0 copy-done.1
  186.1 0.0 copy-start.2
  186.1 1.9 copy-done.2
  188.0 0.0 copy-start.4
  188.0 1.9 copy-done.4
  189.9 4.7 %outer_step.1 = (f32[6272,128]{1,0:T(8,128)}, f32[6272,128]{1,0:T(8,128)}) custom-call(f32[128,128]{1,0:T(8,128)S(1)} %bitcast.13, f32[6272,128]{1,0:T(8,128)S(1)} %copy-done.4, f32[6272,128]{1,0:T(8,128)S(1)} %bitcast.11, f32[6272,128]{1,0:T(8,128)S(1)} %bitcast.12), custom_call_target="tpu_custom_call" | custom-call | tf_op jit(solution)/shard_map/outer_step/pallas_call | solution.py:109
  (2 shorter events, 0.1 us)
Async XLA Ops:
  0.6 4.7 %copy-start = (bf16[1,2,896,3584]{3,2,1,0:T(8,128)(2,1)S(1)}, bf16[1,2,896,3584]{3,2,1,0:T(8,128)(2,1)}, u32[]{:S(2)}) copy-start(bf16[1,2,896,3584]{3,2,1,0:T(8,128)(2,1)} %param.3) | copy-start | bytes 38535172
  165.9 20.2 %copy-start.1 = (f32[2,4,1,1,4,1,28,896]{7,5,6,4,3,2,1,0:T(1,128)S(1)}, f32[2,4,1,1,4,1,28,896]{7,5,6,4,3,2,1,0:T(1,128)}, u32[]{:S(2)}) copy-start(f32[2,4,1,1,4,1,28,896]{7,5,6,4,3,2,1,0:T(1,128)} %param.4) | copy-start | bytes 9633796
  167.9 1.7 copy-start.3
  186.1 1.9 copy-start.2
  188.0 1.9 copy-start.4

commit v2 on v1

--- a/solution.py
+++ b/solution.py
@@ -38,11 +38,11 @@
         out_shape=jax.ShapeDtypeStruct(
             (replicas, rows_split, cols_split, 2 * row_tile, col_tile), deltas.dtype
         ),
-        compiler_params=pltpu.CompilerParams(vmem_limit_bytes=24 << 20),
-    )(deltas)
+        compiler_params=pltpu.CompilerParams(vmem_limit_bytes=8 << 20),
+    )(pltpu.with_memory_space_constraint(deltas, pltpu.HBM))
 
 
-def mean_kernel(replicas, blocks, row_tile, col_tile, x_ref, mean_ref, squares_ref):
+def mean_kernel(replicas, blocks, row_tile, col_tile, x_ref, mean_ref, shared_ref, squares_ref):
     lane_tiles = col_tile // LANES
     squares_ref[...] = jnp.zeros_like(squares_ref)
 
@@ -73,9 +73,12 @@
         return carry
 
     lax.fori_loop(0, blocks, block, 0)
+    shared_ref[...] = jnp.broadcast_to(
+        jnp.sum(squares_ref[...], axis=0, keepdims=True), shared_ref.shape
+    )
 
 
-def average(received, row_tile, col_tile):
+def average(received, devices, row_tile, col_tile):
     replicas, blocks = received.shape[:2]
     size = blocks * 2 * row_tile * col_tile
     return pl.pallas_call(
@@ -85,35 +88,47 @@
         out_specs=[pl.BlockSpec(memory_space=pltpu.VMEM)] * 2,
         out_shape=[
             jax.ShapeDtypeStruct((size // LANES, LANES), jnp.float32),
-            jax.ShapeDtypeStruct((8, LANES), jnp.float32),
+            jax.ShapeDtypeStruct((devices, LANES), jnp.float32),
         ],
-        compiler_params=pltpu.CompilerParams(vmem_limit_bytes=24 << 20),
+        scratch_shapes=[pltpu.VMEM((8, LANES), jnp.float32)],
+        compiler_params=pltpu.CompilerParams(vmem_limit_bytes=4 << 20),
     )(received)
 
 
-def step_kernel(entries, squares_ref, mean_ref, params_ref, momentum_ref, params_out, momentum_out):
+def step_kernel(entries, pieces, squares_ref, mean_ref, params_ref, momentum_ref, params_out, momentum_out, params_new, momentum_new, sems):
     squares = jnp.sum(squares_ref[...], keepdims=True)
     root_mean = jnp.sqrt(squares * (1.0 / entries) + epsilon)
     clip_scale = jnp.minimum(1.0, clip_level / root_mean)
-    gradient = clip_scale * mean_ref[...]
-    momentum = moment_decay * momentum_ref[...] + gradient
-    momentum_out[...] = momentum
-    params_out[...] = params_ref[...] - outer_rate * (gradient + moment_decay * momentum)
+    rows = mean_ref.shape[0] // pieces
+    copies = []
+    for piece in range(pieces):
+        at = pl.ds(piece * rows, rows)
+        gradient = clip_scale * mean_ref[at, :]
+        momentum = moment_decay * momentum_ref[at, :] + gradient
+        momentum_new[at, :] = momentum
+        params_new[at, :] = params_ref[at, :] - outer_rate * (gradient + moment_decay * momentum)
+        for n, (new, out) in enumerate(((momentum_new, momentum_out), (params_new, params_out))):
+            copy = pltpu.make_async_copy(new.at[at], out.at[at], sems.at[n, piece])
+            copy.start()
+            copies.append(copy)
+    for copy in copies:
+        copy.wait()
 
 
 def step(squares, mean, params, momentum, entries):
-    rows = mean.shape[0]
     pieces = 8
-    whole = pl.BlockSpec(squares.shape, lambda i: (0, 0))
-    tile = pl.BlockSpec((rows // pieces, LANES), lambda i: (i, 0))
     return pl.pallas_call(
-        lambda *refs: step_kernel(entries, *refs),
+        lambda *refs: step_kernel(entries, pieces, *refs),
         name="outer_step",
-        grid=(pieces,),
-        in_specs=[whole, tile, tile, tile],
-        out_specs=[tile, tile],
+        in_specs=[pl.BlockSpec(memory_space=pltpu.VMEM)] * 4,
+        out_specs=[pl.BlockSpec(memory_space=pltpu.HBM)] * 2,
         out_shape=[jax.ShapeDtypeStruct(mean.shape, jnp.float32)] * 2,
-        compiler_params=pltpu.CompilerParams(vmem_limit_bytes=16 << 20),
+        scratch_shapes=[
+            pltpu.VMEM(mean.shape, jnp.float32),
+            pltpu.VMEM(mean.shape, jnp.float32),
+            pltpu.SemaphoreType.DMA((2, pieces)),
+        ],
+        compiler_params=pltpu.CompilerParams(vmem_limit_bytes=12 << 20),
     )(squares, mean, params, momentum)
 
 
@@ -130,9 +145,8 @@
     packed = packed.reshape(devices, 2 * row_tile, col_tile)
     received = lax.all_to_all(packed, EVERY, split_axis=0, concat_axis=0, tiled=True)
     received = received.reshape(replicas, rows_split * cols_split, 2 * row_tile, col_tile)
-    mean, squares = average(received, row_tile, col_tile)
-    squares = jnp.sum(squares, axis=0, keepdims=True)
-    squares = jnp.broadcast_to(squares[None], (devices, 1, LANES))
+    mean, squares = average(received, devices, row_tile, col_tile)
+    squares = squares.reshape(devices, 1, LANES)
     squares = lax.all_to_all(squares, EVERY, split_axis=0, concat_axis=0, tiled=True)
     flat = mean.shape
     new_params, new_momentum = step(

time: 195 us -> 191 us (0.979)
  local copies, waits for them, and re-layouts: 10.2 us -> 0.01 us
  Pallas kernels: 10.5 us -> 16.2 us
    unnamed x10 -> x4, local copies, waits for them, and re-layouts: 10.1 us -> 0.01 us
    pallas_call x1, Pallas kernels: 3.77 us -> 11.2 us  [pack(): pl.pallas_call(lambda x_ref, out_ref: pack_kernel(replicas, row_tile, x_r...]
where the time goes in v2:
time: 191 us; the launch traced here: 190 us
  blocking collectives  173 us (91%)
  Pallas kernels  16.2 us (8%)
    all_to_all x1, blocking collectives, per_device(): lax.all_to_all(packed, EVERY, split_axis=0, concat_axis=0, tiled=True)  157 us
    all_to_all x1, blocking collectives, per_device(): lax.all_to_all(squares, EVERY, split_axis=0, concat_axis=0, tiled=True)  16.5 us
    pallas_call x1, Pallas kernels, pack(): pl.pallas_call(lambda x_ref, out_ref: pack_kernel(replicas, row_tile, x_r...  11.2 us

profile of v2, /device:TPU:1, one launch (start us, length us, event | category | flops | bytes accessed | tf_op | source)
XLA Modules:
  0.0 190.1 jit_solution(5660700298143068666)
XLA Ops:
  0.6 11.2 %pack.1 = bf16[8,4,4,56,896]{4,3,2,1,0:T(8,128)(2,1)S(1)} custom-call(bf16[2,896,3584]{2,1,0:T(8,128)(2,1)} %bitcast.17), custom_call_target="tpu_custom_call" | custom-call | tf_op jit(solution)/shard_map/pack/pallas_call | solution.py:30
  11.8 156.8 %all_to_all.10 = bf16[128,56,896]{2,1,0:T(8,128)(2,1)S(1)} all-to-all(bf16[128,56,896]{2,1,0:T(8,128)(2,1)S(1)} %bitcast.12), channel_id=1, replica_groups=mesh['rep_0'=2,'rep_1'=4,'gx_0'=2,'gx_1'=2,'gy'=4] {'rep_0','rep_1','gx_..., dimensions={0} | all-to-all | bytes 25690112 | tf_op jit(solution)/shard_map/all_to_all | solution.py:146
  168.6 0.0 copy-start
  168.6 0.0 copy-start.1
  168.6 2.0 %average.1 = (f32[6272,128]{1,0:T(8,128)S(1)}, f32[128,128]{1,0:T(8,128)S(1)}) custom-call(bf16[8,16,56,896]{3,2,1,0:T(8,128)(2,1)S(1)} %bitcast.11), custom_call_target="tpu_custom_call" | custom-call | tf_op jit(solution)/shard_map/average/pallas_call | solution.py:84
  170.6 16.5 %all_to_all.11 = f32[128,1,128]{2,1,0:T(1,128)S(1)} all-to-all(f32[128,1,128]{2,1,0:T(1,128)S(1)} %bitcast.16), channel_id=1, replica_groups=mesh['rep_0'=2,'rep_1'=4,'gx_0'=2,'gx_1'=2,'gy'=4] {'rep_0','rep_1','gx_..., dimensions={0} | all-to-all | bytes 131072 | tf_op jit(solution)/shard_map/all_to_all | solution.py:150
  187.1 0.0 copy-done
  187.1 0.0 copy-done.1
  187.1 3.0 %outer_step.1 = (f32[6272,128]{1,0:T(8,128)}, f32[6272,128]{1,0:T(8,128)}) custom-call(f32[128,128]{1,0:T(8,128)S(1)} %bitcast.15, f32[6272,128]{1,0:T(8,128)S(1)} %get-tuple-element.7.refs_1_, f32[6272,128]{1,0:T(8,128)S(1)} %bitcast.13, f32[6272,128]{1,0:T(8,128)S(1)} %bitcast.14), custom_call_target="tpu_custom_call" | custom-call | tf_op jit(solution)/shard_map/outer_step/pallas_call | solution.py:120
Async XLA Ops:
  168.6 18.5 %copy-start = (f32[2,4,1,1,4,1,28,896]{7,5,6,4,3,2,1,0:T(1,128)S(1)}, f32[2,4,1,1,4,1,28,896]{7,5,6,4,3,2,1,0:T(1,128)}, u32[]{:S(2)}) copy-start(f32[2,4,1,1,4,1,28,896]{7,5,6,4,3,2,1,0:T(1,128)} %param.4) | copy-start | bytes 9633796
  168.6 18.5 %copy-start.1 = (f32[2,4,1,1,4,1,28,896]{7,5,6,4,3,2,1,0:T(1,128)S(1)}, f32[2,4,1,1,4,1,28,896]{7,5,6,4,3,2,1,0:T(1,128)}, u32[]{:S(2)}) copy-start(f32[2,4,1,1,4,1,28,896]{7,5,6,4,3,2,1,0:T(1,128)} %param.5) | copy-start | bytes 9633796

commit v3 on v2

--- a/solution.py
+++ b/solution.py
@@ -8,7 +8,7 @@
 
 GX = ("gx_0", "gx_1")
 REP = ("rep_0", "rep_1")
-EVERY = ("rep_0", "rep_1", "gx_0", "gx_1", "gy")
+EVERY = ("gy", "rep_1", "rep_0", "gx_0", "gx_1")
 LANES = 128
 
 clip_level = 0.25
@@ -17,43 +17,58 @@
 epsilon = 1e-06
 
 
-def pack_kernel(replicas, row_tile, x_ref, out_ref):
-    for r in range(replicas):
+def pack_kernel(row_tile, x_ref, out_ref, landed, sems):
+    cols_split, inner, outer, rows_split = out_ref.shape[:4]
+    col_tile = out_ref.shape[5]
+    block_rows = outer * inner * row_tile
+    copies = {}
+    for c in range(rows_split):
         for m in range(2):
-            out_ref[r, 0, 0, m * row_tile : (m + 1) * row_tile, :] = x_ref[
-                m, r * row_tile : (r + 1) * row_tile, :
-            ]
+            at = pl.ds(c * block_rows, block_rows)
+            copies[c, m] = pltpu.make_async_copy(
+                x_ref.at[m, at, :], landed.at[m, at, :], sems.at[c, m]
+            )
+            copies[c, m].start()
+    for c in range(rows_split):
+        for m in range(2):
+            copies[c, m].wait()
+            for r in range(outer * inner):
+                row = c * block_rows + r * row_tile
+                for d in range(cols_split):
+                    out_ref[d, r % inner, r // inner, c, m * row_tile : (m + 1) * row_tile, :] = (
+                        landed[m, row : row + row_tile, d * col_tile : (d + 1) * col_tile]
+                    )
 
 
-def pack(deltas, replicas, rows_split, cols_split, row_tile, col_tile):
-    block_rows = replicas * row_tile
+def pack(deltas, slots, row_tile, col_tile):
     return pl.pallas_call(
-        lambda x_ref, out_ref: pack_kernel(replicas, row_tile, x_ref, out_ref),
+        lambda *refs: pack_kernel(row_tile, *refs),
         name="pack",
-        grid=(rows_split, cols_split),
-        in_specs=[pl.BlockSpec((2, block_rows, col_tile), lambda c, d: (0, c, d))],
-        out_specs=pl.BlockSpec(
-            (replicas, 1, 1, 2 * row_tile, col_tile), lambda c, d: (0, c, d, 0, 0)
-        ),
-        out_shape=jax.ShapeDtypeStruct(
-            (replicas, rows_split, cols_split, 2 * row_tile, col_tile), deltas.dtype
-        ),
-        compiler_params=pltpu.CompilerParams(vmem_limit_bytes=8 << 20),
+        in_specs=[pl.BlockSpec(memory_space=pltpu.HBM)],
+        out_specs=pl.BlockSpec(memory_space=pltpu.VMEM),
+        out_shape=jax.ShapeDtypeStruct((*slots, 2 * row_tile, col_tile), deltas.dtype),
+        scratch_shapes=[
+            pltpu.VMEM(deltas.shape, deltas.dtype),
+            pltpu.SemaphoreType.DMA((slots[3], 2)),
+        ],
+        compiler_params=pltpu.CompilerParams(vmem_limit_bytes=16 << 20),
     )(pltpu.with_memory_space_constraint(deltas, pltpu.HBM))
 
 
-def mean_kernel(replicas, blocks, row_tile, col_tile, x_ref, mean_ref, shared_ref, squares_ref):
-    lane_tiles = col_tile // LANES
+def mean_kernel(x_ref, mean_ref, shared_ref, squares_ref):
+    cols_split, inner, outer, rows_split, rows, columns = x_ref.shape
+    row_tile, lane_tiles = rows // 2, columns // LANES
+    blocks = rows_split * cols_split
     squares_ref[...] = jnp.zeros_like(squares_ref)
 
     def block(ab, carry):
-        for group in range(2 * row_tile // 8):
-            total = x_ref[0, ab, group * 8 : group * 8 + 8, :].astype(jnp.float32)
-            for replica in range(1, replicas):
-                total = total + x_ref[
-                    replica, ab, group * 8 : group * 8 + 8, :
-                ].astype(jnp.float32)
-            mean = total * (1.0 / replicas)
+        a, b = ab // cols_split, ab % cols_split
+        for group in range(rows // 8):
+            at = slice(group * 8, group * 8 + 8)
+            total = x_ref[b, 0, 0, a, at, :].astype(jnp.float32)
+            for r in range(1, outer * inner):
+                total = total + x_ref[b, r % inner, r // inner, a, at, :].astype(jnp.float32)
+            mean = total * (1.0 / (outer * inner))
             square = mean * mean
             partial = square[:, :LANES]
             for j in range(1, lane_tiles):
@@ -61,8 +76,7 @@
             squares_ref[...] += partial
             row = 0
             while row < 8:
-                at = group * 8 + row
-                m, i = at // row_tile, at % row_tile
+                m, i = (group * 8 + row) // row_tile, (group * 8 + row) % row_tile
                 count = min(8 - row, row_tile - i)
                 start = ((m * blocks + ab) * row_tile + i) * lane_tiles
                 for j in range(lane_tiles):
@@ -78,16 +92,17 @@
     )
 
 
-def average(received, devices, row_tile, col_tile):
-    replicas, blocks = received.shape[:2]
-    size = blocks * 2 * row_tile * col_tile
+def average(received, devices):
+    cols_split, _, _, rows_split, rows, columns = received.shape
     return pl.pallas_call(
-        lambda *refs: mean_kernel(replicas, blocks, row_tile, col_tile, *refs),
+        mean_kernel,
         name="average",
         in_specs=[pl.BlockSpec(memory_space=pltpu.VMEM)],
         out_specs=[pl.BlockSpec(memory_space=pltpu.VMEM)] * 2,
         out_shape=[
-            jax.ShapeDtypeStruct((size // LANES, LANES), jnp.float32),
+            jax.ShapeDtypeStruct(
+                (cols_split * rows_split * rows * columns // LANES, LANES), jnp.float32
+            ),
             jax.ShapeDtypeStruct((devices, LANES), jnp.float32),
         ],
         scratch_shapes=[pltpu.VMEM((8, LANES), jnp.float32)],
@@ -141,11 +156,16 @@
     row_tile = local_rows // (rows_split * replicas)
     col_tile = local_cols // cols_split
     entries = matrices * local_rows * local_cols * rows_split * cols_split
-    packed = pack(deltas[0], replicas, rows_split, cols_split, row_tile, col_tile)
-    packed = packed.reshape(devices, 2 * row_tile, col_tile)
-    received = lax.all_to_all(packed, EVERY, split_axis=0, concat_axis=0, tiled=True)
-    received = received.reshape(replicas, rows_split * cols_split, 2 * row_tile, col_tile)
-    mean, squares = average(received, devices, row_tile, col_tile)
+    slots = (cols_split, *(lax.axis_size(n) for n in reversed(REP)), rows_split)
+    packed = pack(deltas[0], slots, row_tile, col_tile)
+    received = lax.all_to_all(
+        packed.reshape(devices, 2 * row_tile, col_tile),
+        EVERY,
+        split_axis=0,
+        concat_axis=0,
+        tiled=True,
+    )
+    mean, squares = average(received.reshape(packed.shape), devices)
     squares = squares.reshape(devices, 1, LANES)
     squares = lax.all_to_all(squares, EVERY, split_axis=0, concat_axis=0, tiled=True)
     flat = mean.shape

time: 191 us -> 182 us (0.953)
  Pallas kernels: 16.2 us -> 10.1 us
  blocking collectives: 173 us -> 171 us
    pallas_call x2, Pallas kernels: 13.2 us -> 7.07 us  [the longest x1 4.95 us: pack(): pl.pallas_call(lambda *refs: pack_kernel(row_tile, *refs), name='pack', i...]
    all_to_all x1, blocking collectives: 16.5 us -> 13.8 us  [per_device(): lax.all_to_all(squares, EVERY, split_axis=0, concat_axis=0, tiled=True)]
where the time goes in v3:
time: 182 us
  blocking collectives  171 us (94%)
  Pallas kernels  10.1 us (6%)
    all_to_all x1, blocking collectives, per_device(): lax.all_to_all(packed.reshape(devices, 2 * row_tile, col_tile), EVERY, sp...  157 us
    all_to_all x1, blocking collectives, per_device(): lax.all_to_all(squares, EVERY, split_axis=0, concat_axis=0, tiled=True)  13.8 us
    pallas_call x1, Pallas kernels, pack(): pl.pallas_call(lambda *refs: pack_kernel(row_tile, *refs), name='pack', i...  4.95 us

profile of v3, /device:TPU:1, one launch (start us, length us, event | category | flops | bytes accessed | tf_op | source)
XLA Modules:
  0.0 181.8 jit_solution(6916753357927978091)
XLA Ops:
  0.6 4.9 %pack.1 = bf16[4,4,2,4,56,896]{5,4,3,2,1,0:T(8,128)(2,1)S(1)} custom-call(bf16[2,896,3584]{2,1,0:T(8,128)(2,1)} %bitcast.17), custom_call_target="tpu_custom_call" | custom-call | tf_op jit(solution)/shard_map/pack/pallas_call | solution.py:44
  5.6 157.2 %all_to_all.10 = bf16[128,56,896]{2,1,0:T(8,128)(2,1)S(1)} all-to-all(bf16[128,56,896]{2,1,0:T(8,128)(2,1)S(1)} %bitcast.12), channel_id=1, replica_groups=mesh['rep_0'=2,'rep_1'=4,'gx_0'=2,'gx_1'=2,'gy'=4] {'gy','rep_1','rep_0'..., dimensions={0} | all-to-all | bytes 25690112 | tf_op jit(solution)/shard_map/all_to_all | solution.py:161
  162.8 0.0 copy-start
  162.8 0.0 copy-start.1
  162.8 2.1 %average.1 = (f32[6272,128]{1,0:T(8,128)S(1)}, f32[128,128]{1,0:T(8,128)S(1)}) custom-call(bf16[4,4,2,4,56,896]{5,4,3,2,1,0:T(8,128)(2,1)S(1)} %bitcast.11), custom_call_target="tpu_custom_call" | custom-call | tf_op jit(solution)/shard_map/average/pallas_call | solution.py:97
  164.9 13.8 %all_to_all.11 = f32[128,1,128]{2,1,0:T(1,128)S(1)} all-to-all(f32[128,1,128]{2,1,0:T(1,128)S(1)} %bitcast.16), channel_id=1, replica_groups=mesh['rep_0'=2,'rep_1'=4,'gx_0'=2,'gx_1'=2,'gy'=4] {'gy','rep_1','rep_0'..., dimensions={0} | all-to-all | bytes 131072 | tf_op jit(solution)/shard_map/all_to_all | solution.py:170
  178.8 0.0 copy-done
  178.8 0.0 copy-done.1
  178.8 3.0 %outer_step.1 = (f32[6272,128]{1,0:T(8,128)}, f32[6272,128]{1,0:T(8,128)}) custom-call(f32[128,128]{1,0:T(8,128)S(1)} %bitcast.15, f32[6272,128]{1,0:T(8,128)S(1)} %get-tuple-element.7.refs_1_, f32[6272,128]{1,0:T(8,128)S(1)} %bitcast.13, f32[6272,128]{1,0:T(8,128)S(1)} %bitcast.14), custom_call_target="tpu_custom_call" | custom-call | tf_op jit(solution)/shard_map/outer_step/pallas_call | solution.py:135
Async XLA Ops:
  162.8 16.0 %copy-start = (f32[2,4,1,1,4,1,28,896]{7,5,6,4,3,2,1,0:T(1,128)S(1)}, f32[2,4,1,1,4,1,28,896]{7,5,6,4,3,2,1,0:T(1,128)}, u32[]{:S(2)}) copy-start(f32[2,4,1,1,4,1,28,896]{7,5,6,4,3,2,1,0:T(1,128)} %param.4) | copy-start | bytes 9633796
  162.8 16.0 %copy-start.1 = (f32[2,4,1,1,4,1,28,896]{7,5,6,4,3,2,1,0:T(1,128)S(1)}, f32[2,4,1,1,4,1,28,896]{7,5,6,4,3,2,1,0:T(1,128)}, u32[]{:S(2)}) copy-start(f32[2,4,1,1,4,1,28,896]{7,5,6,4,3,2,1,0:T(1,128)} %param.5) | copy-start | bytes 9633796

commit v4 on v3

--- a/solution.py
+++ b/solution.py
@@ -55,48 +55,46 @@
     )(pltpu.with_memory_space_constraint(deltas, pltpu.HBM))
 
 
-def mean_kernel(x_ref, mean_ref, shared_ref, squares_ref):
+def sum_kernel(x_ref, sum_ref, shared_ref):
     cols_split, inner, outer, rows_split, rows, columns = x_ref.shape
     row_tile, lane_tiles = rows // 2, columns // LANES
     blocks = rows_split * cols_split
-    squares_ref[...] = jnp.zeros_like(squares_ref)
 
-    def block(ab, carry):
+    def block(ab, squares):
         a, b = ab // cols_split, ab % cols_split
         for group in range(rows // 8):
             at = slice(group * 8, group * 8 + 8)
             total = x_ref[b, 0, 0, a, at, :].astype(jnp.float32)
             for r in range(1, outer * inner):
                 total = total + x_ref[b, r % inner, r // inner, a, at, :].astype(jnp.float32)
-            mean = total * (1.0 / (outer * inner))
-            square = mean * mean
+            square = total * total
             partial = square[:, :LANES]
             for j in range(1, lane_tiles):
                 partial = partial + square[:, j * LANES : (j + 1) * LANES]
-            squares_ref[...] += partial
+            squares = squares + partial
             row = 0
             while row < 8:
                 m, i = (group * 8 + row) // row_tile, (group * 8 + row) % row_tile
                 count = min(8 - row, row_tile - i)
                 start = ((m * blocks + ab) * row_tile + i) * lane_tiles
                 for j in range(lane_tiles):
-                    mean_ref[pl.ds(start + j, count, stride=lane_tiles), :] = mean[
+                    sum_ref[pl.ds(start + j, count, stride=lane_tiles), :] = total[
                         row : row + count, j * LANES : (j + 1) * LANES
                     ]
                 row += count
-        return carry
+        return squares
 
-    lax.fori_loop(0, blocks, block, 0)
+    squares = lax.fori_loop(0, blocks, block, jnp.zeros((8, LANES), jnp.float32))
     shared_ref[...] = jnp.broadcast_to(
-        jnp.sum(squares_ref[...], axis=0, keepdims=True), shared_ref.shape
+        jnp.sum(squares, axis=0, keepdims=True), shared_ref.shape
     )
 
 
-def average(received, devices):
+def add_up(received, devices):
     cols_split, _, _, rows_split, rows, columns = received.shape
     return pl.pallas_call(
-        mean_kernel,
-        name="average",
+        sum_kernel,
+        name="add_up",
         in_specs=[pl.BlockSpec(memory_space=pltpu.VMEM)],
         out_specs=[pl.BlockSpec(memory_space=pltpu.VMEM)] * 2,
         out_shape=[
@@ -105,20 +103,18 @@
             ),
             jax.ShapeDtypeStruct((devices, LANES), jnp.float32),
         ],
-        scratch_shapes=[pltpu.VMEM((8, LANES), jnp.float32)],
         compiler_params=pltpu.CompilerParams(vmem_limit_bytes=4 << 20),
     )(received)
 
 
-def step_kernel(entries, pieces, squares_ref, mean_ref, params_ref, momentum_ref, params_out, momentum_out, params_new, momentum_new, sems):
-    squares = jnp.sum(squares_ref[...], keepdims=True)
+def step_kernel(entries, replicas, cuts, squares_ref, sum_ref, params_ref, momentum_ref, params_out, momentum_out, params_new, momentum_new, sems):
+    squares = jnp.sum(squares_ref[...], keepdims=True) * (1.0 / replicas**2)
     root_mean = jnp.sqrt(squares * (1.0 / entries) + epsilon)
-    clip_scale = jnp.minimum(1.0, clip_level / root_mean)
-    rows = mean_ref.shape[0] // pieces
+    sum_scale = jnp.minimum(1.0, clip_level / root_mean) * (1.0 / replicas)
     copies = []
-    for piece in range(pieces):
-        at = pl.ds(piece * rows, rows)
-        gradient = clip_scale * mean_ref[at, :]
+    for piece, (low, high) in enumerate(zip(cuts, cuts[1:])):
+        at = pl.ds(low, high - low)
+        gradient = sum_scale * sum_ref[at, :]
         momentum = moment_decay * momentum_ref[at, :] + gradient
         momentum_new[at, :] = momentum
         params_new[at, :] = params_ref[at, :] - outer_rate * (gradient + moment_decay * momentum)
@@ -130,21 +126,23 @@
         copy.wait()
 
 
-def step(squares, mean, params, momentum, entries):
-    pieces = 8
+def step(squares, total, params, momentum, entries, replicas):
+    tiles = total.shape[0] // 8
+    shares = (1, 2, 4, 4, 4, 4, 4, 4, 1)
+    cuts = [tiles * sum(shares[:n]) // sum(shares) * 8 for n in range(len(shares) + 1)]
     return pl.pallas_call(
-        lambda *refs: step_kernel(entries, pieces, *refs),
+        lambda *refs: step_kernel(entries, replicas, cuts, *refs),
         name="outer_step",
         in_specs=[pl.BlockSpec(memory_space=pltpu.VMEM)] * 4,
         out_specs=[pl.BlockSpec(memory_space=pltpu.HBM)] * 2,
-        out_shape=[jax.ShapeDtypeStruct(mean.shape, jnp.float32)] * 2,
+        out_shape=[jax.ShapeDtypeStruct(total.shape, jnp.float32)] * 2,
         scratch_shapes=[
-            pltpu.VMEM(mean.shape, jnp.float32),
-            pltpu.VMEM(mean.shape, jnp.float32),
-            pltpu.SemaphoreType.DMA((2, pieces)),
+            pltpu.VMEM(total.shape, jnp.float32),
+            pltpu.VMEM(total.shape, jnp.float32),
+            pltpu.SemaphoreType.DMA((2, len(shares))),
         ],
         compiler_params=pltpu.CompilerParams(vmem_limit_bytes=12 << 20),
-    )(squares, mean, params, momentum)
+    )(squares, total, params, momentum)
 
 
 def per_device(deltas, params, momentum):
@@ -165,12 +163,12 @@
         concat_axis=0,
         tiled=True,
     )
-    mean, squares = average(received.reshape(packed.shape), devices)
+    total, squares = add_up(received.reshape(packed.shape), devices)
     squares = squares.reshape(devices, 1, LANES)
     squares = lax.all_to_all(squares, EVERY, split_axis=0, concat_axis=0, tiled=True)
-    flat = mean.shape
+    flat = total.shape
     new_params, new_momentum = step(
-        squares.reshape(devices, LANES), mean, params.reshape(flat), momentum.reshape(flat), entries
+        squares.reshape(devices, LANES), total, params.reshape(flat), momentum.reshape(flat), entries, replicas
     )
     return new_params.reshape(params.shape), new_momentum.reshape(params.shape)
 

time: 182 us -> 182 us (level)
  no operation moved by 1% of the time
where the time goes in v4:
time: 182 us
  blocking collectives  171 us (94%)
  Pallas kernels  9.95 us (5%)
    all_to_all x1, blocking collectives, per_device(): lax.all_to_all(packed.reshape(devices, 2 * row_tile, col_tile), EVERY, sp...  157 us
    all_to_all x1, blocking collectives, per_device(): lax.all_to_all(squares, EVERY, split_axis=0, concat_axis=0, tiled=True)  13.8 us
    pallas_call x1, Pallas kernels, pack(): pl.pallas_call(lambda *refs: pack_kernel(row_tile, *refs), name='pack', i...  4.95 us

profile of v4, /device:TPU:1, one launch (start us, length us, event | category | flops | bytes accessed | tf_op | source)
XLA Modules:
  0.0 181.7 jit_solution(16641687826574092668)
XLA Ops:
  0.6 4.9 %pack.1 = bf16[4,4,2,4,56,896]{5,4,3,2,1,0:T(8,128)(2,1)S(1)} custom-call(bf16[2,896,3584]{2,1,0:T(8,128)(2,1)} %bitcast.17), custom_call_target="tpu_custom_call" | custom-call | tf_op jit(solution)/shard_map/pack/pallas_call | solution.py:44
  5.6 157.2 %all_to_all.10 = bf16[128,56,896]{2,1,0:T(8,128)(2,1)S(1)} all-to-all(bf16[128,56,896]{2,1,0:T(8,128)(2,1)S(1)} %bitcast.12), channel_id=1, replica_groups=mesh['rep_0'=2,'rep_1'=4,'gx_0'=2,'gx_1'=2,'gy'=4] {'gy','rep_1','rep_0'..., dimensions={0} | all-to-all | bytes 25690112 | tf_op jit(solution)/shard_map/all_to_all | solution.py:159
  162.8 0.0 copy-start
  162.8 0.0 copy-start.1
  162.8 2.0 %add_up.1 = (f32[6272,128]{1,0:T(8,128)S(1)}, f32[128,128]{1,0:T(8,128)S(1)}) custom-call(bf16[4,4,2,4,56,896]{5,4,3,2,1,0:T(8,128)(2,1)S(1)} %bitcast.11), custom_call_target="tpu_custom_call" | custom-call | tf_op jit(solution)/shard_map/add_up/pallas_call | solution.py:95
  164.8 13.8 %all_to_all.11 = f32[128,1,128]{2,1,0:T(1,128)S(1)} all-to-all(f32[128,1,128]{2,1,0:T(1,128)S(1)} %bitcast.16), channel_id=1, replica_groups=mesh['rep_0'=2,'rep_1'=4,'gx_0'=2,'gx_1'=2,'gy'=4] {'gy','rep_1','rep_0'..., dimensions={0} | all-to-all | bytes 131072 | tf_op jit(solution)/shard_map/all_to_all | solution.py:168
  178.7 0.0 copy-done
  178.7 0.0 copy-done.1
  178.7 3.0 %outer_step.1 = (f32[6272,128]{1,0:T(8,128)}, f32[6272,128]{1,0:T(8,128)}) custom-call(f32[128,128]{1,0:T(8,128)S(1)} %bitcast.15, f32[6272,128]{1,0:T(8,128)S(1)} %get-tuple-element.7.refs_1_, f32[6272,128]{1,0:T(8,128)S(1)} %bitcast.13, f32[6272,128]{1,0:T(8,128)S(1)} %bitcast.14), custom_call_target="tpu_custom_call" | custom-call | tf_op jit(solution)/shard_map/outer_step/pallas_call | solution.py:133
Async XLA Ops:
  162.8 15.9 %copy-start = (f32[2,4,1,1,4,1,28,896]{7,5,6,4,3,2,1,0:T(1,128)S(1)}, f32[2,4,1,1,4,1,28,896]{7,5,6,4,3,2,1,0:T(1,128)}, u32[]{:S(2)}) copy-start(f32[2,4,1,1,4,1,28,896]{7,5,6,4,3,2,1,0:T(1,128)} %param.4) | copy-start | bytes 9633796
  162.8 15.9 %copy-start.1 = (f32[2,4,1,1,4,1,28,896]{7,5,6,4,3,2,1,0:T(1,128)S(1)}, f32[2,4,1,1,4,1,28,896]{7,5,6,4,3,2,1,0:T(1,128)}, u32[]{:S(2)}) copy-start(f32[2,4,1,1,4,1,28,896]{7,5,6,4,3,2,1,0:T(1,128)} %param.5) | copy-start | bytes 9633796
